TPU v7x, 32 devices: a whole 2x2x4 slice. The times are simulated.
32 devices in a mesh: mem: 16 (over z, y, x), row: 2 (over core).
Axes of the slice: x: 2, y: 2, z: 4, core: 2. Of those that a mesh axis runs over, the one named last changes fastest.
Arguments:
- realization_stack: float32 [16, 5, 32, 256], P('mem', None, 'row'), may hold values from -6 to 6
- velocity: float32 [2, 32, 256], P(None, 'row'), may hold values from -0.25 to 0.25
- diffusion: float32 [5], replicated, may hold values from 0.04 to 0.12
- obs_cell: int32 [2048], replicated, may hold values from 0 to 40959
- obs_order: int32 [2048], replicated, may hold values from 0 to 2047, each once
- obs_value: float32 [2048], replicated, may hold values from -6 to 6
- obs_var: float32 [2048], replicated, may hold values from 0.2 to 2
- field_mask: int32 [5, 5], replicated, may hold values 0 or 1
Outputs:
- analysis: float32 [16, 5, 2, 16, 256], P(None, None, 'row', 'mem')
Inputs may be any that keep to these rules, and one draw needn't show every extreme that they name: `obs_cell`: a flat index field * 32 * 256 + row * 256 + column. `obs_order`: each of 0 to 2047 exactly once.
All inputs are finite; a program needn't handle non-finite values.
Results may differ from a plain program's by a relative error of at most 0.0003.
Values sent between devices are 32-bit elements; how exact they have to be, the bound alone decides.
No kernel may reach another device: no remote copies, remote signals or barrier semaphores. Data moves between devices by JAX's collectives and lax.ppermute only.
A program may use at most 64 MiB of HBM per device.

v0:
```python
import jax
import jax.numpy as jnp
from jax import lax
from jax.sharding import PartitionSpec as P

SUBSTEPS = 4
BATCHES = 2
LOC_HALF = 32
precise = lax.Precision.HIGHEST


def extended(shard, sides, width):
    for axis, dim in sides:
        count, length = (lax.axis_size(axis), shard.shape[dim])
        up = [(i, (i + 1) % count) for i in range(count - 1)]
        down = [(j, i) for i, j in up]
        last = lax.slice_in_dim(shard, length - width, length, axis=dim)
        initial = lax.slice_in_dim(shard, 0, width, axis=dim)
        before = lax.ppermute(last, axis, up)
        after = lax.ppermute(initial, axis, down)
        shard = jnp.concatenate([before, shard, after], axis=dim)
    return shard


def advance(padded, velocity, diffusion):
    spec_pad = ((0, 0),) * (padded.ndim - 1) + ((1, 1),)
    col_padded = jnp.pad(padded, spec_pad)
    centre = col_padded[..., 1:-1, 1:-1]
    north_cell = col_padded[..., :-2, 1:-1]
    south_cell = col_padded[..., 2:, 1:-1]
    west_cell = col_padded[..., 1:-1, :-2]
    east_cell = col_padded[..., 1:-1, 2:]
    along_col = velocity[0]
    along_row = velocity[1]
    spread = north_cell + south_cell + west_cell + east_cell - 4.0 * centre
    carried = (
        jnp.maximum(along_col, 0.0) * (centre - west_cell)
        + jnp.minimum(along_col, 0.0) * (east_cell - centre)
        + jnp.maximum(along_row, 0.0) * (centre - north_cell)
        + jnp.minimum(along_row, 0.0) * (south_cell - centre)
    )
    return centre + diffusion[:, None, None] * spread - carried


def gaspari(dist_sq):
    scaled = jnp.sqrt(dist_sq) / LOC_HALF
    clipped = jnp.maximum(scaled, 1.0)
    inner_part = (
        ((-0.25 * scaled + 0.5) * scaled + 0.625) * scaled - 5.0 / 3.0
    ) * scaled * scaled + 1.0
    outer_part = (
        ((((scaled / 12.0 - 0.5) * scaled + 0.625) * scaled + 5.0 / 3.0) * scaled - 5.0) * scaled
        + 4.0
        - 2.0 / (3.0 * clipped)
    )
    return jnp.where(scaled <= 1.0, inner_part, jnp.where(scaled <= 2.0, outer_part, 0.0))


def decode(flat_cells, total_rows, n_cols):
    field_ids = flat_cells // (total_rows * n_cols)
    row_ids = flat_cells // n_cols % total_rows
    col_ids = flat_cells % n_cols
    return (field_ids, row_ids, col_ids)


def innovations(priors, obs_values, obs_noise):
    members = priors.shape[0]
    average = jnp.mean(priors, axis=0)
    anomaly = priors - average
    spread = jnp.sum(anomaly * anomaly, axis=0) / (members - 1)
    variance_sum = spread + obs_noise
    root_sum = jnp.sqrt(variance_sum)
    shrink = 1.0 / (root_sum * (jnp.sqrt(obs_noise) + root_sum))
    adjust = (obs_values - average) / variance_sum - shrink * anomaly
    return (anomaly, adjust)


def regress(
    ensemble_now, base_row, obs_field, obs_row, obs_col, anomaly, adjust, field_mask, n_cols
):
    members, n_cells = ensemble_now.shape
    n_fields = field_mask.shape[0]
    per_field = n_cells // n_fields
    local_ids = lax.iota(jnp.int32, per_field)
    cell_row = (base_row + local_ids // n_cols).astype(jnp.float32)
    cell_col = (local_ids % n_cols).astype(jnp.float32)
    centred = ensemble_now - jnp.mean(ensemble_now, axis=0)
    mask_float = field_mask.astype(jnp.float32)
    total_obs = obs_field.shape[0]
    obs_block = min(256, total_obs)
    increment = jnp.zeros_like(ensemble_now)
    for offset in range(0, total_obs, obs_block):
        row_gap = cell_row[:, None] - obs_row[None, offset : offset + obs_block].astype(jnp.float32)
        col_gap = cell_col[:, None] - obs_col[None, offset : offset + obs_block].astype(jnp.float32)
        closeness = gaspari(row_gap * row_gap + col_gap * col_gap)
        field_hot = (
            obs_field[None, offset : offset + obs_block] == lax.iota(jnp.int32, n_fields)[:, None]
        ).astype(jnp.float32)
        allowed = jnp.dot(mask_float, field_hot, precision=precise)
        covariance = lax.dot_general(
            centred,
            anomaly[:, offset : offset + obs_block],
            (((0,), (0,)), ((), ())),
            precision=precise,
        )
        weights = (
            covariance.reshape(n_fields, per_field, obs_block)
            * (closeness[None] * allowed[:, None, :])
            / (members - 1)
        )
        increment = increment + lax.dot_general(
            adjust[:, offset : offset + obs_block],
            weights.reshape(n_cells, obs_block),
            (((1,), (1,)), ((), ())),
            precision=precise,
        )
    return ensemble_now + increment


def per_device(
    realization_stack, velocity, diffusion, obs_cell, obs_order, obs_value, obs_var, field_mask
):
    local_members = realization_stack.shape[0]
    n_fields = realization_stack.shape[1]
    rows_here = realization_stack.shape[2]
    n_cols = realization_stack.shape[3]
    n_mem = lax.axis_size("mem")
    n_slab = lax.axis_size("row")
    total_members = local_members * n_mem
    total_rows = rows_here * n_slab
    slab_index = lax.axis_index("row")
    member_index = lax.axis_index("mem")
    row_sub = rows_here // n_mem
    current = realization_stack
    for substep in range(SUBSTEPS):
        padded = extended(current, (("row", 2),), 1)
        current = advance(padded, velocity, diffusion)
    field_all, row_all, col_all = decode(obs_cell, total_rows, n_cols)
    batch_size = obs_cell.shape[0] // BATCHES
    layout = lax.all_to_all(current, "mem", split_axis=2, concat_axis=0, tiled=True)
    ensemble_now = layout.reshape(total_members, -1)
    base_row = slab_index * rows_here + member_index * row_sub
    for batch_num in range(BATCHES):
        picked = obs_order[batch_num * batch_size : (batch_num + 1) * batch_size]
        obs_field = field_all[picked]
        obs_row = row_all[picked]
        obs_col = col_all[picked]
        owned = ((obs_row >= base_row) & (obs_row < base_row + row_sub)).astype(jnp.float32)
        local_ids = (
            obs_field * row_sub * n_cols
            + jnp.clip(obs_row - base_row, 0, row_sub - 1) * n_cols
            + obs_col
        )
        partial_priors = jnp.take(ensemble_now, local_ids, axis=1) * owned[None, :]
        priors = lax.psum(partial_priors, ("mem", "row"))
        anomaly, adjust = innovations(priors, obs_value[picked], obs_var[picked])
        ensemble_now = regress(
            ensemble_now, base_row, obs_field, obs_row, obs_col, anomaly, adjust, field_mask, n_cols
        )
    return ensemble_now.reshape(total_members, n_fields, 1, row_sub, n_cols)


def solution(mesh):
    in_specs = (P("mem", None, "row", None), P(None, "row", None), P(), P(), P(), P(), P(), P())
    out_specs = P(None, None, "row", "mem", None)
    return jax.shard_map(
        per_device, mesh=mesh, in_specs=in_specs, out_specs=out_specs, check_vma=False
    )
```

profile of v0, /device:TPU:0, one launch (start us, length us, event | category | flops | bytes accessed | tf_op | source)
XLA Modules:
  0.0 403.0 jit_solution(6026265140585205028)
XLA Ops:
  7.5 1.3 collective-permute-start.1
  8.8 3.0 collective-permute-start
  13.3 6.1 %gather_fusion.8 = s32[1024]{0:T(1024)S(1)} fusion(s32[2048]{0:T(1024)S(1)} %get-tuple-element.33, s32[1024]{0:T(1024)S(1)} %get-tuple-element.28), kind=kCustom, calls=%fused_computation.10 | custom fusion | bytes 12288 | tf_op jit(solution)/shard_map/gather | solution.py:147
  19.4 6.2 %gather_fusion.7 = s32[1024]{0:T(1024)S(1)} fusion(s32[2048]{0:T(1024)S(1)} %get-tuple-element.32, s32[1024]{0:T(1024)S(1)} %get-tuple-element.28), kind=kCustom, calls=%fused_computation.9 | custom fusion | bytes 12288 | tf_op jit(solution)/shard_map/gather | solution.py:146
  25.6 6.2 %gather_fusion.3 = s32[1024]{0:T(1024)S(1)} fusion(s32[2048]{0:T(1024)S(1)} %get-tuple-element.33, s32[1024]{0:T(1024)S(1)} %get-tuple-element.29), kind=kCustom, calls=%fused_computation.5 | custom fusion | bytes 12288 | tf_op jit(solution)/shard_map/gather | solution.py:147
  31.8 6.2 %gather_fusion.2 = s32[1024]{0:T(1024)S(1)} fusion(s32[2048]{0:T(1024)S(1)} %get-tuple-element.32, s32[1024]{0:T(1024)S(1)} %get-tuple-element.29), kind=kCustom, calls=%fused_computation.4 | custom fusion | bytes 12288 | tf_op jit(solution)/shard_map/gather | solution.py:146
  37.9 6.2 %gather_fusion.1 = s32[1024]{0:T(1024)S(1)} fusion(s32[2048]{0:T(1024)S(1)} %get-tuple-element.34, s32[1024]{0:T(1024)S(1)} %get-tuple-element.29), kind=kCustom, calls=%fused_computation.3 | custom fusion | bytes 12288 | tf_op jit(solution)/shard_map/gather | solution.py:145
  44.1 6.2 %gather_fusion.6 = s32[1024]{0:T(1024)S(1)} fusion(s32[2048]{0:T(1024)S(1)} %get-tuple-element.34, s32[1024]{0:T(1024)S(1)} %get-tuple-element.28), kind=kCustom, calls=%fused_computation.8 | custom fusion | bytes 12288 | tf_op jit(solution)/shard_map/gather | solution.py:145
  51.1 3.7 fusion.25
  55.0 1.7 broadcast_multiply_fusion
  57.2 1.3 collective-permute-start.3
  58.5 3.0 collective-permute-start.2
  62.6 1.3 collective-permute-start.5
  63.9 3.0 collective-permute-start.4
  68.0 1.3 collective-permute-start.7
  69.3 3.0 collective-permute-start.6
  72.4 6.2 %gather_fusion = f32[1024]{0:T(1024)S(1)} fusion(f32[2048]{0:T(1024)S(1)} %copy-done, s32[1024]{0:T(1024)S(1)} %get-tuple-element.29), kind=kCustom, calls=%fused_computation.2 | custom fusion | bytes 12288 | tf_op jit(solution)/shard_map/gather | solution.py:156
  78.6 6.2 %gather_fusion.5 = f32[1024]{0:T(1024)S(1)} fusion(f32[2048]{0:T(1024)S(1)} %copy-done, s32[1024]{0:T(1024)S(1)} %get-tuple-element.28), kind=kCustom, calls=%fused_computation.7 | custom fusion | bytes 12288 | tf_op jit(solution)/shard_map/gather | solution.py:156
  84.7 6.2 %gather_fusion.4 = f32[1024]{0:T(1024)S(1)} fusion(f32[2048]{0:T(1024)S(1)} %copy-done.1, s32[1024]{0:T(1024)S(1)} %get-tuple-element.29), kind=kCustom, calls=%fused_computation.6 | custom fusion | bytes 12288 | tf_op jit(solution)/shard_map/gather | solution.py:156
  90.9 6.2 %gather_fusion.9 = f32[1024]{0:T(1024)S(1)} fusion(f32[2048]{0:T(1024)S(1)} %copy-done.1, s32[1024]{0:T(1024)S(1)} %get-tuple-element.28), kind=kCustom, calls=%fused_computation.11 | custom fusion | bytes 12288 | tf_op jit(solution)/shard_map/gather | solution.py:156
  98.0 8.3 %all-to-all-start = ((f32[1,5,16,256]{3,1,0,2:T(8,128)}), f32[1,5,16,256]{3,1,0,2:T(8,128)S(1)}, u32[]{:S(2)}, u32[]{:S(2)}) async-start(f32[1,5,16,256]{3,1,0,2:T(8,128)} %fusion.48), calls=%async_computation | async-start | bytes 262144 | tf_op jit(solution)/shard_map/all_to_all | solution.py:140
  106.4 7.7 %all-to-all-done = f32[1,5,16,256]{3,1,0,2:T(8,128)S(1)} async-done(((f32[1,5,16,256]{3,1,0,2:T(8,128)}), f32[1,5,16,256]{3,1,0,2:T(8,128)S(1)}, u32[]{:S(2)}, u32[]{:S(2)}) %all-to-all-start) | async-done | bytes 81952 | tf_op jit(solution)/shard_map/all_to_all | solution.py:140
  114.4 4.0 gather_fusion.10
  120.6 114.6 %all-reduce.7.cloned.1.call-done = f32[16,1024]{1,0:T(8,128)} async-done(((f32[16,1024]{1,0:T(8,128)}), f32[16,1024]{1,0:T(8,128)}) %all-reduce.7.cloned.1.call-update) | async-done | bytes 65552 | tf_op jit(solution)/shard_map/psum | solution.py:155
  247.1 4.2 %gather_fusion.11 = f32[1024,16]{1,0:T(8,128)} fusion(f32[16,1280]{0,1:T(8,128)S(1)} %copy.44, s32[1024]{0:T(1024)S(1)} %broadcast_clamp_fusion), kind=kCustom, calls=%fused_computation.1.clone | custom fusion | bytes 135168 | tf_op jit(solution)/shard_map/jit(_take)/gather | solution.py:154
  251.3 2.2 bitcast_multiply_fusion
  253.5 128.8 %all-reduce.9.cloned.1.call-done = f32[16,1024]{0,1:T(8,128)} async-done(((f32[16,1024]{0,1:T(8,128)}), f32[16,1024]{0,1:T(8,128)}) %all-reduce.9.cloned.1.call-update) | async-done | bytes 65552 | tf_op jit(solution)/shard_map/psum | solution.py:155
  383.5 1.4 multiply_reduce_fusion
  384.9 1.3 fusion
  391.7 1.3 convolution_add_fusion.2
  392.9 1.3 convolution_add_fusion.1
  394.2 1.3 fusion.4
  (102 shorter events, 28.5 us)
Async XLA Ops:
  6.5 65.8 %copy-start = (f32[2048]{0:T(1024)S(1)}, f32[2048]{0:T(1024)}, u32[]{:S(2)}) copy-start(f32[2048]{0:T(1024)} %param.15) | copy-start | bytes 24580
  7.5 49.4 %collective-permute-start.1 = (f32[1,5,1,256]{3,1,0,2:T(8,128)S(1)}, f32[1,5,1,256]{3,1,0,2:T(8,128)S(1)}, u32[]{:S(2)}, u32[]{:S(2)}) collective-permute-start(f32[1,5,1,256]{3,1,0,2:T(8,128)S(1)} %get-tuple-element.21), channel_id=1, source_target_pairs={{1,0},{3,2},{5,4},{7,6},{9,8},{11,10},{13,12},{15,14},{17,16},{19,... | collective-permute-start | bytes 15368 | tf_op jit(solution)/shard_map/ppermute | solution.py:20
  8.8 48.1 %collective-permute-start = (f32[1,5,1,256]{3,1,0,2:T(8,128)S(1)}, f32[1,5,1,256]{3,1,0,2:T(8,128)S(1)}, u32[]{:S(2)}, u32[]{:S(2)}) collective-permute-start(f32[1,5,1,256]{3,1,0,2:T(8,128)S(1)} %get-tuple-element.20), channel_id=1, source_target_pairs={{0,1},{2,3},{4,5},{6,7},{8,9},{10,11},{12,13},{14,15},{16,17},{18,... | collective-permute-start | bytes 15368 | tf_op jit(solution)/shard_map/ppermute | solution.py:19
  44.1 6.2 %copy-start.9 = (f32[2,16,256]{2,1,0:T(8,128)S(1)}, f32[2,16,256]{2,1,0:T(8,128)}, u32[]{:S(2)}) copy-start(f32[2,16,256]{2,1,0:T(8,128)} %param.11) | copy-start | bytes 98308
  44.1 6.3 %copy-start.8 = (s32[5,5]{1,0:T(8,128)S(1)}, s32[5,5]{1,0:T(8,128)}, u32[]{:S(2)}) copy-start(s32[5,5]{1,0:T(8,128)} %param.17) | copy-start | bytes 304
  55.0 2.0 copy-start.10
  57.2 4.5 %collective-permute-start.3 = (f32[1,5,1,256]{3,1,0,2:T(8,128)S(1)}, f32[1,5,1,256]{3,1,0,2:T(8,128)S(1)}, u32[]{:S(2)}, u32[]{:S(2)}) collective-permute-start(f32[1,5,1,256]{3,1,0,2:T(8,128)S(1)} %get-tuple-element.19), channel_id=1, source_target_pairs={{1,0},{3,2},{5,4},{7,6},{9,8},{11,10},{13,12},{15,14},{17,16},{19,... | collective-permute-start | bytes 15368 | tf_op jit(solution)/shard_map/ppermute | solution.py:20
  58.5 3.8 collective-permute-start.2
  62.6 4.5 %collective-permute-start.5 = (f32[1,5,1,256]{3,1,0,2:T(8,128)S(1)}, f32[1,5,1,256]{3,1,0,2:T(8,128)S(1)}, u32[]{:S(2)}, u32[]{:S(2)}) collective-permute-start(f32[1,5,1,256]{3,1,0,2:T(8,128)S(1)} %get-tuple-element.17), channel_id=1, source_target_pairs={{1,0},{3,2},{5,4},{7,6},{9,8},{11,10},{13,12},{15,14},{17,16},{19,... | collective-permute-start | bytes 15368 | tf_op jit(solution)/shard_map/ppermute | solution.py:20
  63.9 3.8 collective-permute-start.4
  68.0 29.0 %collective-permute-start.7 = (f32[1,5,1,256]{3,1,0,2:T(8,128)S(1)}, f32[1,5,1,256]{3,1,0,2:T(8,128)S(1)}, u32[]{:S(2)}, u32[]{:S(2)}) collective-permute-start(f32[1,5,1,256]{3,1,0,2:T(8,128)S(1)} %get-tuple-element.15), channel_id=1, source_target_pairs={{1,0},{3,2},{5,4},{7,6},{9,8},{11,10},{13,12},{15,14},{17,16},{19,... | collective-permute-start | bytes 15368 | tf_op jit(solution)/shard_map/ppermute | solution.py:20
  69.3 27.7 %collective-permute-start.6 = (f32[1,5,1,256]{3,1,0,2:T(8,128)S(1)}, f32[1,5,1,256]{3,1,0,2:T(8,128)S(1)}, u32[]{:S(2)}, u32[]{:S(2)}) collective-permute-start(f32[1,5,1,256]{3,1,0,2:T(8,128)S(1)} %get-tuple-element.14), channel_id=1, source_target_pairs={{0,1},{2,3},{4,5},{6,7},{8,9},{10,11},{12,13},{14,15},{16,17},{18,... | collective-permute-start | bytes 15368 | tf_op jit(solution)/shard_map/ppermute | solution.py:19
  78.6 6.2 %copy-start.1 = (f32[2048]{0:T(1024)S(1)}, f32[2048]{0:T(1024)}, u32[]{:S(2)}) copy-start(f32[2048]{0:T(1024)} %param.16) | copy-start | bytes 24580
  98.0 16.1 %all-to-all-start = ((f32[1,5,16,256]{3,1,0,2:T(8,128)}), f32[1,5,16,256]{3,1,0,2:T(8,128)S(1)}, u32[]{:S(2)}, u32[]{:S(2)}) async-start(f32[1,5,16,256]{3,1,0,2:T(8,128)} %fusion.48), calls=%async_computation | async-start | bytes 262144 | tf_op jit(solution)/shard_map/all_to_all | solution.py:140
  106.3 128.8 %all-reduce.7.cloned.1.call-start = ((), (), s32[]{:S(2)}) async-start(), calls=%async_computation.1 | async-start | bytes 131072 | tf_op jit(solution)/shard_map/psum | solution.py:155
  118.4 118.5 %copy-start.7 = (f32[256,256]{1,0:T(8,128)S(1)}, f32[256,256]{1,0:T(8,128)}, u32[]{:S(2)}) copy-start(f32[256,256]{1,0:T(8,128)} %get-tuple-element.68) | copy-start | bytes 786436
  120.3 261.9 %all-reduce.9.cloned.1.call-start = ((), (), s32[]{:S(2)}) async-start(), calls=%async_computation.2 | async-start | bytes 1048576 | tf_op jit(solution)/shard_map/psum | solution.py:155
  236.9 2.5 copy-start.6
  239.4 2.5 copy-start.5
  241.9 2.5 copy-start.4
  386.2 1.3 copy-start.3
  387.5 1.3 copy-start.2
Sparse Core Ops, SparseCore 0:
  120.5 114.6 all-reduce.6
  253.6 128.6 all-reduce.8
where the time goes:
time: 404 us; the launch traced here: 403 us
  waiting for transfers between devices  253 us (63%)
  local copies, waits for them, and re-layouts  73.4 us (18%)
  starting transfers between devices  25.9 us (6%)
  matrix products  20.7 us (5%)
  other arithmetic  16.5 us (4%)
  between operations  14.1 us (3%)
    psum x2, waiting for transfers between devices, per_device(): priors = lax.psum(partial_priors, ('mem', 'row'))  243 us
    gather x4, local copies, waits for them, and re-layouts, per_device(): anomaly, adjust = innovations(priors, obs_value[picked], obs_var[picked])  24.6 us
    gather x2, local copies, waits for them, and re-layouts, per_device(): obs_field = field_all[picked]  12.3 us
    gather x2, local copies, waits for them, and re-layouts, per_device(): obs_row = row_all[picked]  12.3 us
    gather x2, local copies, waits for them, and re-layouts, per_device(): obs_col = col_all[picked]  12.3 us
    ppermute x4, starting transfers between devices, extended(): before = lax.ppermute(last, axis, up)  12.1 us
    dot_general x8, matrix products, regress(): lax.dot_general(centred, anomaly[:, offset:offset + obs_block], (((0,), (...  9.99 us
    dot_general x8, matrix products, regress(): lax.dot_general(adjust[:, offset:offset + obs_block], weights.reshape(n_c...  9.76 us
  transfers between devices with their start and end apart: 11, of which 5 were waited for; matrix products, arithmetic and copies ran while one was open for 17% of the time, Pallas kernels for 0%

commit v1 on v0

--- a/solution.py
+++ b/solution.py
@@ -152,7 +152,7 @@
             + obs_col
         )
         partial_priors = jnp.take(ensemble_now, local_ids, axis=1) * owned[None, :]
-        priors = lax.psum(partial_priors, ("mem", "row"))
+        priors = jnp.sum(lax.all_gather(partial_priors, ("mem", "row")), axis=0)
         anomaly, adjust = innovations(priors, obs_value[picked], obs_var[picked])
         ensemble_now = regress(
             ensemble_now, base_row, obs_field, obs_row, obs_col, anomaly, adjust, field_mask, n_cols

time: 404 us -> 237 us (0.59)
  waiting for transfers between devices: 253 us -> 86 us
    psum x2 -> x0, waiting for transfers between devices: 243 us -> none  [per_device(): priors = lax.psum(partial_priors, ('mem', 'row'))]
    all_gather x0 -> x2, waiting for transfers between devices: none -> 76.5 us  [per_device(): priors = jnp.sum(lax.all_gather(partial_priors, ('mem', 'row')), axis=0)]
    reduce_sum x0 -> x2, other arithmetic: none -> 4.33 us  [per_device(): priors = jnp.sum(lax.all_gather(partial_priors, ('mem', 'row')), axis=0)]
    gather x3 -> x4, local copies, waits for them, and re-layouts: 9.46 us -> 5.96 us  [per_device(): partial_priors = jnp.take(ensemble_now, local_ids, axis=1) * owned[None, :]]
  transfers between devices with their start and end apart: 11 -> 11, of which waited for: 5 -> 6; matrix products, arithmetic and copies ran while one was open for 17% -> 30% of each run, Pallas kernels for 0% -> 0%
where the time goes in v1:
time: 237 us; the launch traced here: 236 us
  waiting for transfers between devices  86 us (36%)
  local copies, waits for them, and re-layouts  70.5 us (30%)
  starting transfers between devices  25.9 us (11%)
  matrix products  22.7 us (10%)
  other arithmetic  16.9 us (7%)
  between operations  14.1 us (6%)
    all_gather x2, waiting for transfers between devices, per_device(): priors = jnp.sum(lax.all_gather(partial_priors, ('mem', 'row')), axis=0)  76.5 us
    gather x4, local copies, waits for them, and re-layouts, per_device(): anomaly, adjust = innovations(priors, obs_value[picked], obs_var[picked])  24.8 us
    gather x2, local copies, waits for them, and re-layouts, per_device(): obs_col = col_all[picked]  12.3 us
    gather x2, local copies, waits for them, and re-layouts, per_device(): obs_row = row_all[picked]  12.3 us
    gather x2, local copies, waits for them, and re-layouts, per_device(): obs_field = field_all[picked]  12.3 us
    dot_general x8, matrix products, regress(): lax.dot_general(centred, anomaly[:, offset:offset + obs_block], (((0,), (...  12.2 us
    ppermute x4, starting transfers between devices, extended(): before = lax.ppermute(last, axis, up)  12.1 us
    dot_general x8, matrix products, regress(): lax.dot_general(adjust[:, offset:offset + obs_block], weights.reshape(n_c...  9.47 us
  transfers between devices with their start and end apart: 11, of which 6 were waited for; matrix products, arithmetic and copies ran while one was open for 30% of the time, Pallas kernels for 0%

profile of v1, /device:TPU:0, one launch (start us, length us, event | category | flops | bytes accessed | tf_op | source)
XLA Modules:
  0.0 236.0 jit_solution(7131072668330672747)
XLA Ops:
  7.5 1.3 collective-permute-start.1
  8.8 3.0 %collective-permute-start = (f32[1,5,1,256]{3,1,0,2:T(8,128)S(1)}, f32[1,5,1,256]{3,1,0,2:T(8,128)S(1)}, u32[]{:S(2)}, u32[]{:S(2)}) collective-permute-start(f32[1,5,1,256]{3,1,0,2:T(8,128)S(1)} %get-tuple-element.20), channel_id=1, source_target_pairs={{0,1},{2,3},{4,5},{6,7},{8,9},{10,11},{12,13},{14,15},{16,17},{18,... | collective-permute-start | bytes 15368 | tf_op jit(solution)/shard_map/ppermute | solution.py:19
  13.6 1.3 collective-permute-start.3
  14.9 3.0 %collective-permute-start.2 = (f32[1,5,1,256]{3,1,0,2:T(8,128)S(1)}, f32[1,5,1,256]{3,1,0,2:T(8,128)S(1)}, u32[]{:S(2)}, u32[]{:S(2)}) collective-permute-start(f32[1,5,1,256]{3,1,0,2:T(8,128)S(1)} %get-tuple-element.18), channel_id=1, source_target_pairs={{0,1},{2,3},{4,5},{6,7},{8,9},{10,11},{12,13},{14,15},{16,17},{18,... | collective-permute-start | bytes 15368 | tf_op jit(solution)/shard_map/ppermute | solution.py:19
  19.1 1.3 collective-permute-start.5
  20.4 3.0 %collective-permute-start.4 = (f32[1,5,1,256]{3,1,0,2:T(8,128)S(1)}, f32[1,5,1,256]{3,1,0,2:T(8,128)S(1)}, u32[]{:S(2)}, u32[]{:S(2)}) collective-permute-start(f32[1,5,1,256]{3,1,0,2:T(8,128)S(1)} %get-tuple-element.16), channel_id=1, source_target_pairs={{0,1},{2,3},{4,5},{6,7},{8,9},{10,11},{12,13},{14,15},{16,17},{18,... | collective-permute-start | bytes 15368 | tf_op jit(solution)/shard_map/ppermute | solution.py:19
  23.4 6.2 %gather_fusion.8 = s32[1024]{0:T(1024)S(1)} fusion(s32[2048]{0:T(1024)S(1)} %get-tuple-element.33, s32[1024]{0:T(1024)S(1)} %get-tuple-element.28), kind=kCustom, calls=%fused_computation.10 | custom fusion | bytes 12288 | tf_op jit(solution)/shard_map/gather | solution.py:147
  29.6 6.2 %gather_fusion.7 = s32[1024]{0:T(1024)S(1)} fusion(s32[2048]{0:T(1024)S(1)} %get-tuple-element.32, s32[1024]{0:T(1024)S(1)} %get-tuple-element.28), kind=kCustom, calls=%fused_computation.9 | custom fusion | bytes 12288 | tf_op jit(solution)/shard_map/gather | solution.py:146
  35.7 6.2 %gather_fusion.3 = s32[1024]{0:T(1024)S(1)} fusion(s32[2048]{0:T(1024)S(1)} %get-tuple-element.33, s32[1024]{0:T(1024)S(1)} %get-tuple-element.29), kind=kCustom, calls=%fused_computation.5 | custom fusion | bytes 12288 | tf_op jit(solution)/shard_map/gather | solution.py:147
  41.9 6.2 %gather_fusion.2 = s32[1024]{0:T(1024)S(1)} fusion(s32[2048]{0:T(1024)S(1)} %get-tuple-element.32, s32[1024]{0:T(1024)S(1)} %get-tuple-element.29), kind=kCustom, calls=%fused_computation.4 | custom fusion | bytes 12288 | tf_op jit(solution)/shard_map/gather | solution.py:146
  48.1 6.2 %gather_fusion.1 = s32[1024]{0:T(1024)S(1)} fusion(s32[2048]{0:T(1024)S(1)} %get-tuple-element.34, s32[1024]{0:T(1024)S(1)} %get-tuple-element.29), kind=kCustom, calls=%fused_computation.3 | custom fusion | bytes 12288 | tf_op jit(solution)/shard_map/gather | solution.py:145
  54.2 6.2 %gather_fusion.6 = s32[1024]{0:T(1024)S(1)} fusion(s32[2048]{0:T(1024)S(1)} %get-tuple-element.34, s32[1024]{0:T(1024)S(1)} %get-tuple-element.28), kind=kCustom, calls=%fused_computation.8 | custom fusion | bytes 12288 | tf_op jit(solution)/shard_map/gather | solution.py:145
  60.7 1.3 collective-permute-start.7
  62.0 3.0 %collective-permute-start.6 = (f32[1,5,1,256]{3,1,0,2:T(8,128)S(1)}, f32[1,5,1,256]{3,1,0,2:T(8,128)S(1)}, u32[]{:S(2)}, u32[]{:S(2)}) collective-permute-start(f32[1,5,1,256]{3,1,0,2:T(8,128)S(1)} %get-tuple-element.14), channel_id=1, source_target_pairs={{0,1},{2,3},{4,5},{6,7},{8,9},{10,11},{12,13},{14,15},{16,17},{18,... | collective-permute-start | bytes 15368 | tf_op jit(solution)/shard_map/ppermute | solution.py:19
  66.8 8.3 %all-to-all-start = ((f32[1,5,16,256]{3,1,0,2:T(8,128)}), f32[1,5,16,256]{3,1,0,2:T(8,128)S(1)}, u32[]{:S(2)}, u32[]{:S(2)}) async-start(f32[1,5,16,256]{3,1,0,2:T(8,128)} %fusion.39), calls=%async_computation | async-start | bytes 262144 | tf_op jit(solution)/shard_map/all_to_all | solution.py:140
  75.1 7.9 %all-to-all-done = f32[1,5,16,256]{3,1,0,2:T(8,128)S(1)} async-done(((f32[1,5,16,256]{3,1,0,2:T(8,128)}), f32[1,5,16,256]{3,1,0,2:T(8,128)S(1)}, u32[]{:S(2)}, u32[]{:S(2)}) %all-to-all-start) | async-done | bytes 81952 | tf_op jit(solution)/shard_map/all_to_all | solution.py:140
  83.3 2.8 %gather_fusion.10 = f32[1024,16]{1,0:T(8,128)S(1)} fusion(f32[16,1280]{0,1:T(8,128)S(1)} %copy.78, s32[1024]{0:T(1024)S(1)} %broadcast_clamp_fusion.1), kind=kCustom, calls=%fused_computation.clone | custom fusion | bytes 135168 | tf_op jit(solution)/shard_map/jit(_take)/gather | solution.py:154
  87.2 6.2 %gather_fusion = f32[1024]{0:T(1024)S(1)} fusion(f32[2048]{0:T(1024)S(1)} %copy-done, s32[1024]{0:T(1024)S(1)} %get-tuple-element.29), kind=kCustom, calls=%fused_computation.2 | custom fusion | bytes 12288 | tf_op jit(solution)/shard_map/gather | solution.py:156
  93.4 6.2 %gather_fusion.4 = f32[1024]{0:T(1024)S(1)} fusion(f32[2048]{0:T(1024)S(1)} %copy-done.1, s32[1024]{0:T(1024)S(1)} %get-tuple-element.29), kind=kCustom, calls=%fused_computation.6 | custom fusion | bytes 12288 | tf_op jit(solution)/shard_map/gather | solution.py:156
  100.2 3.7 %fusion.25 = (f32[256,256]{1,0:T(8,128)S(1)}, f32[256,256]{1,0:T(8,128)}, f32[256,256]{1,0:T(8,128)}, f32[256,256]{1,0:T(8,128)}, f32[256,256]{1,0:T(8,128)S(1)}...) fusion(f32[256]{0:T(256)S(1)} %get-tuple-element.39, f32[256]{0:T(256)S(1)} %get-tuple-element.35, ...), kind=kLoop, calls=%fused_computation.73 | loop fusion | flops 17301504 | bytes 2115584 | tf_op jit(solution)/shard_map/jit(_where)/select_n | solution.py:56
  103.9 37.2 %all-gather.5.cloned.1.call-done = f32[512,1024]{1,0:T(8,128)} async-done(((f32[16,1024]{1,0:T(8,128)}), f32[512,1024]{1,0:T(8,128)}) %all-gather.5.cloned.1.call-update) | async-done | bytes 2097168 | tf_op jit(solution)/shard_map/all_gather | solution.py:155
  141.1 1.9 reduce_sum.73
  143.5 2.2 fusion.9
  147.0 1.2 fusion.8
  154.6 2.8 %gather_fusion.11 = f32[1024,16]{1,0:T(8,128)S(1)} fusion(f32[16,1280]{0,1:T(8,128)S(1)} %copy.84, s32[1024]{0:T(1024)S(1)} %broadcast_clamp_fusion), kind=kCustom, calls=%fused_computation.1.clone | custom fusion | bytes 135168 | tf_op jit(solution)/shard_map/jit(_take)/gather | solution.py:154
  158.2 6.4 %gather_fusion.5 = f32[1024]{0:T(1024)S(1)} fusion(f32[2048]{0:T(1024)S(1)} %copy-done, s32[1024]{0:T(1024)S(1)} %get-tuple-element.28), kind=kCustom, calls=%fused_computation.7 | custom fusion | bytes 12288 | tf_op jit(solution)/shard_map/gather | solution.py:156
  164.6 6.2 %gather_fusion.9 = f32[1024]{0:T(1024)S(1)} fusion(f32[2048]{0:T(1024)S(1)} %copy-done.1, s32[1024]{0:T(1024)S(1)} %get-tuple-element.28), kind=kCustom, calls=%fused_computation.11 | custom fusion | bytes 12288 | tf_op jit(solution)/shard_map/gather | solution.py:156
  171.3 1.3 broadcast_multiply_fusion.2
  172.6 1.7 broadcast_multiply_fusion
  174.4 39.3 %all-gather.7.cloned.1.call-done = f32[512,1024]{1,0:T(8,128)} async-done(((f32[16,1024]{1,0:T(8,128)}), f32[512,1024]{1,0:T(8,128)}) %all-gather.7.cloned.1.call-update) | async-done | bytes 2097168 | tf_op jit(solution)/shard_map/all_gather | solution.py:155
  213.7 2.5 %reduce_sum.77 = f32[16,1024]{1,0:T(8,128)} reduce(f32[32,16,1024]{2,1,0:T(8,128)} %bitcast.78, f32[]{:T(128)} %constant.177.clone.1), dimensions={0}, to_apply=%region_5.7 | reduce | flops 507904 | bytes 2162692 | tf_op jit(solution)/shard_map/reduce_sum | solution.py:155
  217.2 2.6 %fusion = f32[1280,256]{1,0:T(8,128)S(1)} fusion(f32[1280,256]{1,0:T(8,128)} %bitcast.80, f32[16,1280]{1,0:T(8,128)S(1)} %get-tuple-element.70, f32[1280]{0:T(1024)S(1)} %broadcast_multiply_fusion.4, f32[16,1024]{1,0:T(8,128)S(1)} %get-tuple-element.7), kind=kOutput, calls=%fused_computation.16 | convolution fusion | flops 63590400 | bytes 2727936 | tf_op jit(solution)/shard_map/dot_general | solution.py:100
  (109 shorter events, 27.4 us)
Async XLA Ops:
  6.5 80.7 %copy-start = (f32[2048]{0:T(1024)S(1)}, f32[2048]{0:T(1024)}, u32[]{:S(2)}) copy-start(f32[2048]{0:T(1024)} %param.15) | copy-start | bytes 24580
  6.5 12.4 %copy-start.12 = (f32[5]{0:T(128)S(1)}, f32[5]{0:T(128)}, u32[]{:S(2)}) copy-start(f32[5]{0:T(128)} %param.12) | copy-start | bytes 64
  6.5 11.4 %copy-start.11 = (s32[2048]{0:T(1024)S(1)}, s32[2048]{0:T(1024)}, u32[]{:S(2)}) copy-start(s32[2048]{0:T(1024)} %param.13) | copy-start | bytes 24580
  6.5 16.8 %copy-start.10 = (s32[2048]{0:T(1024)S(1)}, s32[2048]{0:T(1024)}, u32[]{:S(2)}) copy-start(s32[2048]{0:T(1024)} %param.14) | copy-start | bytes 24580
  7.5 5.1 %collective-permute-start.1 = (f32[1,5,1,256]{3,1,0,2:T(8,128)S(1)}, f32[1,5,1,256]{3,1,0,2:T(8,128)S(1)}, u32[]{:S(2)}, u32[]{:S(2)}) collective-permute-start(f32[1,5,1,256]{3,1,0,2:T(8,128)S(1)} %get-tuple-element.21), channel_id=1, source_target_pairs={{1,0},{3,2},{5,4},{7,6},{9,8},{11,10},{13,12},{15,14},{17,16},{19,... | collective-permute-start | bytes 15368 | tf_op jit(solution)/shard_map/ppermute | solution.py:20
  8.8 3.8 %collective-permute-start = (f32[1,5,1,256]{3,1,0,2:T(8,128)S(1)}, f32[1,5,1,256]{3,1,0,2:T(8,128)S(1)}, u32[]{:S(2)}, u32[]{:S(2)}) collective-permute-start(f32[1,5,1,256]{3,1,0,2:T(8,128)S(1)} %get-tuple-element.20), channel_id=1, source_target_pairs={{0,1},{2,3},{4,5},{6,7},{8,9},{10,11},{12,13},{14,15},{16,17},{18,... | collective-permute-start | bytes 15368 | tf_op jit(solution)/shard_map/ppermute | solution.py:19
  13.6 4.4 %collective-permute-start.3 = (f32[1,5,1,256]{3,1,0,2:T(8,128)S(1)}, f32[1,5,1,256]{3,1,0,2:T(8,128)S(1)}, u32[]{:S(2)}, u32[]{:S(2)}) collective-permute-start(f32[1,5,1,256]{3,1,0,2:T(8,128)S(1)} %get-tuple-element.19), channel_id=1, source_target_pairs={{1,0},{3,2},{5,4},{7,6},{9,8},{11,10},{13,12},{15,14},{17,16},{19,... | collective-permute-start | bytes 15368 | tf_op jit(solution)/shard_map/ppermute | solution.py:20
  14.9 3.8 %collective-permute-start.2 = (f32[1,5,1,256]{3,1,0,2:T(8,128)S(1)}, f32[1,5,1,256]{3,1,0,2:T(8,128)S(1)}, u32[]{:S(2)}, u32[]{:S(2)}) collective-permute-start(f32[1,5,1,256]{3,1,0,2:T(8,128)S(1)} %get-tuple-element.18), channel_id=1, source_target_pairs={{0,1},{2,3},{4,5},{6,7},{8,9},{10,11},{12,13},{14,15},{16,17},{18,... | collective-permute-start | bytes 15368 | tf_op jit(solution)/shard_map/ppermute | solution.py:19
  19.1 41.3 %collective-permute-start.5 = (f32[1,5,1,256]{3,1,0,2:T(8,128)S(1)}, f32[1,5,1,256]{3,1,0,2:T(8,128)S(1)}, u32[]{:S(2)}, u32[]{:S(2)}) collective-permute-start(f32[1,5,1,256]{3,1,0,2:T(8,128)S(1)} %get-tuple-element.17), channel_id=1, source_target_pairs={{1,0},{3,2},{5,4},{7,6},{9,8},{11,10},{13,12},{15,14},{17,16},{19,... | collective-permute-start | bytes 15368 | tf_op jit(solution)/shard_map/ppermute | solution.py:20
  20.4 40.1 %collective-permute-start.4 = (f32[1,5,1,256]{3,1,0,2:T(8,128)S(1)}, f32[1,5,1,256]{3,1,0,2:T(8,128)S(1)}, u32[]{:S(2)}, u32[]{:S(2)}) collective-permute-start(f32[1,5,1,256]{3,1,0,2:T(8,128)S(1)} %get-tuple-element.16), channel_id=1, source_target_pairs={{0,1},{2,3},{4,5},{6,7},{8,9},{10,11},{12,13},{14,15},{16,17},{18,... | collective-permute-start | bytes 15368 | tf_op jit(solution)/shard_map/ppermute | solution.py:19
  60.7 4.4 %collective-permute-start.7 = (f32[1,5,1,256]{3,1,0,2:T(8,128)S(1)}, f32[1,5,1,256]{3,1,0,2:T(8,128)S(1)}, u32[]{:S(2)}, u32[]{:S(2)}) collective-permute-start(f32[1,5,1,256]{3,1,0,2:T(8,128)S(1)} %get-tuple-element.15), channel_id=1, source_target_pairs={{1,0},{3,2},{5,4},{7,6},{9,8},{11,10},{13,12},{15,14},{17,16},{19,... | collective-permute-start | bytes 15368 | tf_op jit(solution)/shard_map/ppermute | solution.py:20
  62.0 3.8 %collective-permute-start.6 = (f32[1,5,1,256]{3,1,0,2:T(8,128)S(1)}, f32[1,5,1,256]{3,1,0,2:T(8,128)S(1)}, u32[]{:S(2)}, u32[]{:S(2)}) collective-permute-start(f32[1,5,1,256]{3,1,0,2:T(8,128)S(1)} %get-tuple-element.14), channel_id=1, source_target_pairs={{0,1},{2,3},{4,5},{6,7},{8,9},{10,11},{12,13},{14,15},{16,17},{18,... | collective-permute-start | bytes 15368 | tf_op jit(solution)/shard_map/ppermute | solution.py:19
  66.8 16.3 %all-to-all-start = ((f32[1,5,16,256]{3,1,0,2:T(8,128)}), f32[1,5,16,256]{3,1,0,2:T(8,128)S(1)}, u32[]{:S(2)}, u32[]{:S(2)}) async-start(f32[1,5,16,256]{3,1,0,2:T(8,128)} %fusion.39), calls=%async_computation | async-start | bytes 262144 | tf_op jit(solution)/shard_map/all_to_all | solution.py:140
  75.1 66.0 %all-gather.5.cloned.1.call-start = ((), (), s32[]{:S(2)}) async-start(), calls=%async_computation.1 | async-start | bytes 2162688 | tf_op jit(solution)/shard_map/all_gather | solution.py:155
  87.0 6.4 %copy-start.1 = (f32[2048]{0:T(1024)S(1)}, f32[2048]{0:T(1024)}, u32[]{:S(2)}) copy-start(f32[2048]{0:T(1024)} %param.16) | copy-start | bytes 24580
  87.0 126.7 %all-gather.7.cloned.1.call-start = ((), (), s32[]{:S(2)}) async-start(), calls=%async_computation.2 | async-start | bytes 2162688 | tf_op jit(solution)/shard_map/all_gather | solution.py:155
  93.4 6.3 %copy-start.9 = (s32[5,5]{1,0:T(8,128)S(1)}, s32[5,5]{1,0:T(8,128)}, u32[]{:S(2)}) copy-start(s32[5,5]{1,0:T(8,128)} %param.17) | copy-start | bytes 304
  141.1 2.2 copy-start.2
  143.5 3.4 %copy-start.8 = (f32[256,256]{1,0:T(8,128)S(1)}, f32[256,256]{1,0:T(8,128)}, u32[]{:S(2)}) copy-start(f32[256,256]{1,0:T(8,128)} %get-tuple-element.62) | copy-start | bytes 786436
  147.0 2.5 %copy-start.7 = (f32[256,256]{1,0:T(8,128)S(1)}, f32[256,256]{1,0:T(8,128)}, u32[]{:S(2)}) copy-start(f32[256,256]{1,0:T(8,128)} %get-tuple-element.63) | copy-start | bytes 786436
  149.4 2.4 %copy-start.6 = (f32[256,256]{1,0:T(8,128)S(1)}, f32[256,256]{1,0:T(8,128)}, u32[]{:S(2)}) copy-start(f32[256,256]{1,0:T(8,128)} %get-tuple-element.64) | copy-start | bytes 786436
  213.7 2.5 %copy-start.3 = (f32[512,1024]{1,0:T(8,128)S(1)}, f32[512,1024]{1,0:T(8,128)}, u32[]{:S(2)}) copy-start(f32[512,1024]{1,0:T(8,128)} %all-gather.7.cloned.1.call-done) | copy-start | bytes 6291460
  219.7 1.3 copy-start.5
  221.1 1.3 copy-start.4
Sparse Core Ops, SparseCore 0:
  87.1 53.9 all-gather.4
  158.3 55.2 all-gather.6
